TPU v7x, 32 devices: a whole 2x2x4 slice. The times are simulated.
32 devices in a mesh: replica: 2 (over core), shard: 16 (over z, y, x).
Axes of the slice: x: 2, y: 2, z: 4, core: 2. Of those that a mesh axis runs over, the one named last changes fastest.
Arguments:
- inner_params: bfloat16 [2, 15360, 4096], P('replica', 'shard'), may hold values from -6 to 6
- anchor: float32 [15360, 4096], P('shard'), may hold values from -6 to 6
- momentum: float32 [15360, 4096], P('shard'), may hold values from -2 to 2
- first_moment: bfloat16 [2, 15360, 4096], P('replica', 'shard'), may hold values from -0.59765625 to 0.59765625
- second_moment: bfloat16 [2, 15360, 4096], P('replica', 'shard'), may hold values from 0.0009994507 to 0.099609375
- activations: bfloat16 [2, 64, 4096], P('replica', 'shard'), may hold values from -6 to 6
- cotangent: bfloat16 [2, 15360, 64], P('replica', 'shard'), may hold values from -6 to 6
- spare_index: int32 [16], P('shard'), may hold values from 0 to 1
- peer_index: int32 [16], P('shard'), may hold values from 0 to 1
Outputs:
- anchor_new: float32 [15360, 4096], P('shard')
- momentum_new: float32 [15360, 4096], P('shard')
- update: float32 [2, 15360, 4096], P('replica', 'shard')
Inputs may be any that keep to these rules, and one draw needn't show every extreme that they name: `spare_index`: a replica index for each block. `peer_index`: a replica index for each block; where it equals spare_index the spare keeps its own moments.
All inputs are finite; a program needn't handle non-finite values.
Results may differ from a plain program's by a relative error of at most 0.0018.
Values may be sent and summed in bfloat16 or wider, within the bound.
No kernel may reach another device: no remote copies, remote signals or barrier semaphores. Data moves between devices by JAX's collectives and lax.ppermute only.
A program may use at most 192 MiB of HBM per device.

v0:
```python
import math
import jax
import jax.numpy as jnp
from jax import lax
from jax.sharding import PartitionSpec as P

outer_rate = 0.7
nesterov_mu = 0.9
beta_one = 0.9
beta_two = 0.95
bias_one = 1.0 - 0.9**40
bias_two = 1.0 - 0.95**40
adam_eps = 1e-08
decay_rate = 0.1


def from_root(block, axis, holder):
    block = jnp.where(lax.axis_index(axis) == holder, block, jnp.zeros_like(block))
    return lax.psum(block, axis)


def slope(pre):
    sigma = jax.nn.sigmoid(pre)
    return sigma * (1.0 + pre * (1.0 - sigma))


def local(
    inner_params,
    anchor,
    momentum,
    first_moment,
    second_moment,
    activations,
    cotangent,
    spare_index,
    peer_index,
):
    replicas = lax.axis_size("replica")
    position = lax.axis_index("replica")
    spare_slot = spare_index[0]
    peer_slot = peer_index[0]
    healthy = (position != spare_slot).astype(jnp.float32)
    difference = (anchor - inner_params[0].astype(jnp.float32)) * healthy
    summed = lax.psum(difference, "replica")
    average = summed / (replicas - 1)
    momentum_new = nesterov_mu * momentum + average
    anchor_new = anchor - outer_rate * (average + nesterov_mu * momentum_new)
    received = (
        from_root(first_moment, "replica", peer_slot),
        from_root(second_moment, "replica", peer_slot),
    )
    is_spare = position == spare_slot
    first_used = jnp.where(is_spare, received[0], first_moment)[0].astype(jnp.float32)
    second_used = jnp.where(is_spare, received[1], second_moment)[0].astype(jnp.float32)
    weights = anchor_new.astype(jnp.bfloat16)
    root = math.sqrt(weights.shape[1])
    cot_local = cotangent[0]
    tokens_part = lax.all_gather(activations, "shard", axis=1, tiled=True)[0]
    pre = (
        lax.dot_general(
            weights, tokens_part, (((1,), (1,)), ((), ())), preferred_element_type=jnp.float32
        )
        / root
    )
    grad_pre = (cot_local.astype(jnp.float32) * slope(pre)).astype(jnp.bfloat16)
    gradient = jnp.dot(grad_pre, tokens_part, preferred_element_type=jnp.float32) / root
    first = beta_one * first_used + (1.0 - beta_one) * gradient
    second = beta_two * second_used + (1.0 - beta_two) * gradient * gradient
    update = first / bias_one / (jnp.sqrt(second / bias_two) + adam_eps) + decay_rate * anchor_new
    return (anchor_new, momentum_new, update[None])


def solution(mesh):
    placed = (
        P("replica", "shard", None),
        P("shard", None),
        P("shard", None),
        P("replica", "shard", None),
        P("replica", "shard", None),
        P("replica", "shard", None),
        P("replica", "shard", None),
        P("shard"),
        P("shard"),
    )
    return jax.shard_map(
        local,
        mesh=mesh,
        in_specs=placed,
        out_specs=(P("shard", None), P("shard", None), P("replica", "shard", None)),
        check_vma=False,
    )
```

profile of v0, /device:TPU:0, one launch (start us, length us, event | category | flops | bytes accessed | tf_op | source)
XLA Modules:
  0.0 182.1 jit_solution(2626076116855206710)
XLA Ops:
  7.2 0.0 all-reduce.4.cloned.1.call-start
  7.9 13.2 %fusion = f32[960,4096]{1,0:T(8,128)} fusion(f32[960,4096]{1,0:T(8,128)} %param.10, bf16[1,960,4096]{2,1,0:T(8,128)(2,1)} %param.9, f32[]{:T(128)S(6)} %convert_element_type.31), kind=kLoop, calls=%fused_computation.1 | loop fusion | flops 11796480 | bytes 39321604 | tf_op jit(solution)/shard_map/mul | solution.py:43
  21.1 0.0 all-reduce.4.cloned.1.call-update
  21.1 0.0 all-reduce.6.cloned.1.call-start
  21.8 5.7 %broadcast_select_fusion = (bf16[1,960,4096]{2,1,0:T(8,128)(2,1)}, bf16[1,960,4096]{2,1,0:T(8,128)(2,1)}) fusion(bf16[1,960,4096]{2,1,0:T(8,128)(2,1)} %param.13, pred[]{:T(512)S(6)} %eq.8, bf16[1,960,4096]{2,1,0:T(8,128)(2,1)} %param.12), kind=kLoop, calls=%fused_computation.15 | loop fusion | flops 7864320 | bytes 31457280 | tf_op jit(solution)/shard_map/jit(_where)/select_n | solution.py:18
  27.5 0.0 copy-start
  27.5 0.0 all-reduce.6.cloned.1.call-update
  27.6 0.7 copy-done
  28.3 0.1 copy.13
  28.4 57.0 %all_gather.3 = bf16[1,64,4096]{2,0,1:T(2,128)(2,1)S(1)} all-gather(bf16[1,4,4096]{2,0,1:T(2,128)(2,1)S(1)} %copy.13), channel_id=1, replica_groups=mesh['replica'=2,'shard'=16] {'shard'}, dimensions={1}, use_global_device_ids=true | all-gather | bytes 557056 | tf_op jit(solution)/shard_map/all_gather | solution.py:58
  85.3 0.0 copy-start.1
  85.3 0.0 all-reduce.4.cloned.1.call-done
  85.3 32.9 %multiply_subtract_fusion = (f32[960,4096]{1,0:T(8,128)}, f32[960,4096]{1,0:T(8,128)}) fusion(f32[960,4096]{1,0:T(8,128)} %param.10, f32[960,4096]{1,0:T(8,128)} %all-reduce.4.cloned.1.call-done, f32[960,4096]{1,0:T(8,128)} %param.11), kind=kLoop, calls=%fused_computation.11 | loop fusion | flops 23592960 | bytes 78643200 | tf_op jit(solution)/shard_map/sub | solution.py:47
  118.2 21.2 %all-reduce.6.cloned.1.call-done = (bf16[1,960,4096]{2,1,0:T(8,128)(2,1)}, bf16[1,960,4096]{2,1,0:T(8,128)(2,1)}) async-done(((bf16[1,960,4096]{2,1,0:T(8,128)(2,1)}, bf16[1,960,4096]{2,1,0:T(8,128)(2,1)}), (bf16[1,960,4096]{2,1,0:T(8,128)(2,1)}, bf16[1,960,4096]{2,1,0:T(8,128)(2,1)})) %all-reduce.6.cloned.1.call-update) | async-done | bytes 15728656 | tf_op jit(solution)/shard_map/psum | solution.py:19
  139.5 0.0 copy-done.1
  139.5 35.8 %fusion.6 = f32[1,960,4096]{2,1,0:T(8,128)} fusion(f32[960,4096]{1,0:T(8,128)} %get-tuple-element.5, bf16[1,960,4096]{2,1,0:T(8,128)(2,1)} %get-tuple-element.3, bf16[1,960,4096]{2,1,0:T(8,128)(2,1)} %param.13, bf16[1,960,4096]{2,1,0:T(8,128)(2,1)} %get-tuple-element.4, bf16[1,960,4096]{2,1,0:T(8,128)(2,1)} %param.12, pred[]{:T(512)S(6)} %eq.7, ...), kind=kOutput, calls=%fused_computation.8 | convolution fusion | flops 1082019840 | bytes 63561728 | tf_op jit(solution)/shard_map/dot_general | solution.py:66
Async XLA Ops:
  7.2 78.2 %all-reduce.4.cloned.1.call-start = ((), (), s32[]{:S(2)}) async-start(), calls=%async_computation | async-start | bytes 31457280 | tf_op jit(solution)/shard_map/psum | solution.py:44
  21.1 118.4 %all-reduce.6.cloned.1.call-start = ((), (), s32[]{:S(2)}) async-start(), calls=%async_computation.1 | async-start | bytes 31457280 | tf_op jit(solution)/shard_map/psum | solution.py:19
  27.5 0.8 copy-start
  85.3 54.1 %copy-start.1 = (bf16[1,960,64]{1,2,0:T(8,128)(2,1)S(1)}, bf16[1,960,64]{1,2,0:T(8,128)(2,1)}, u32[]{:S(2)}) copy-start(bf16[1,960,64]{1,2,0:T(8,128)(2,1)} %param.15) | copy-start | bytes 368644
Sparse Core Ops, SparseCore 0:
  21.2 58.5 all-reduce.3
  82.4 57.0 all-reduce.5
where the time goes:
time: 182 us
  blocking collectives  57 us (31%)
  other arithmetic  51.9 us (29%)
  matrix products  35.8 us (20%)
  waiting for transfers between devices  21.3 us (12%)
  between operations  15.4 us (8%)
    all_gather x1, blocking collectives, local(): tokens_part = lax.all_gather(activations, 'shard', axis=1, tiled=True)[0]  57 us
    dot_general x1, matrix products, local(): jnp.dot(grad_pre, tokens_part, preferred_element_type=jnp.float32) / root  35.8 us
    sub x1, other arithmetic, local(): anchor_new = anchor - outer_rate * (average + nesterov_mu * momentum_new)  32.9 us
    psum x1, waiting for transfers between devices, from_root(): return lax.psum(block, axis)  21.2 us
    mul x1, other arithmetic, local(): difference = (anchor - inner_params[0].astype(jnp.float32)) * healthy  13.2 us
    select_n x1, other arithmetic, from_root(): jnp.where(lax.axis_index(axis) == holder, block, jnp.zeros_like(block))  5.75 us
  transfers between devices with their start and end apart: 2, of which 1 were waited for; matrix products, arithmetic and copies ran while one was open for 21% of the time, Pallas kernels for 0%

commit v1 on v0

--- a/solution.py
+++ b/solution.py
@@ -55,7 +55,7 @@
     weights = anchor_new.astype(jnp.bfloat16)
     root = math.sqrt(weights.shape[1])
     cot_local = cotangent[0]
-    tokens_part = lax.all_gather(activations, "shard", axis=1, tiled=True)[0]
+    tokens_part = jnp.concatenate(lax.all_gather(activations, "shard"), axis=1)[0]
     pre = (
         lax.dot_general(
             weights, tokens_part, (((1,), (1,)), ((), ())), preferred_element_type=jnp.float32

time: 182 us -> 182 us (level)
  waiting for transfers between devices: 21.3 us -> 25.9 us
  blocking collectives: 57 us -> 53.1 us
    psum x1, waiting for transfers between devices: 21.2 us -> 25.9 us  [from_root(): return lax.psum(block, axis)]
    all_gather x1, blocking collectives: 57 us -> 53.1 us  [local(): lax.all_gather(activations, 'shard')]
where the time goes in v1:
time: 182 us; the launch traced here: 181 us
  blocking collectives  53.1 us (29%)
  other arithmetic  50.9 us (28%)
  matrix products  35.2 us (19%)
  waiting for transfers between devices  25.9 us (14%)
  between operations  15.4 us (8%)
    all_gather x1, blocking collectives, local(): lax.all_gather(activations, 'shard')  53.1 us
    dot_general x1, matrix products, local(): jnp.dot(grad_pre, tokens_part, preferred_element_type=jnp.float32) / root  35.2 us
    sub x1, other arithmetic, local(): anchor_new = anchor - outer_rate * (average + nesterov_mu * momentum_new)  32 us
    psum x1, waiting for transfers between devices, from_root(): return lax.psum(block, axis)  25.9 us
    mul x1, other arithmetic, local(): difference = (anchor - inner_params[0].astype(jnp.float32)) * healthy  13.2 us
    select_n x1, other arithmetic, from_root(): jnp.where(lax.axis_index(axis) == holder, block, jnp.zeros_like(block))  5.75 us
  transfers between devices with their start and end apart: 2, of which 1 were waited for; matrix products, arithmetic and copies ran while one was open for 21% of the time, Pallas kernels for 0%

profile of v1, /device:TPU:0, one launch (start us, length us, event | category | flops | bytes accessed | tf_op | source)
XLA Modules:
  0.0 181.5 jit_solution(2473547470315777378)
XLA Ops:
  7.2 0.0 all-reduce.4.cloned.1.call-start
  7.9 13.2 %fusion = f32[960,4096]{1,0:T(8,128)} fusion(f32[960,4096]{1,0:T(8,128)} %param.10, bf16[1,960,4096]{2,1,0:T(8,128)(2,1)} %param.9, f32[]{:T(128)S(6)} %convert_element_type.31), kind=kLoop, calls=%fused_computation.1 | loop fusion | flops 11796480 | bytes 39321604 | tf_op jit(solution)/shard_map/mul | solution.py:43
  21.1 0.0 all-reduce.4.cloned.1.call-update
  21.1 0.0 all-reduce.6.cloned.1.call-start
  21.8 5.7 %broadcast_select_fusion = (bf16[1,960,4096]{2,1,0:T(8,128)(2,1)}, bf16[1,960,4096]{2,1,0:T(8,128)(2,1)}) fusion(bf16[1,960,4096]{2,1,0:T(8,128)(2,1)} %param.13, pred[]{:T(512)S(6)} %eq.8, bf16[1,960,4096]{2,1,0:T(8,128)(2,1)} %param.12), kind=kLoop, calls=%fused_computation.15 | loop fusion | flops 7864320 | bytes 31457280 | tf_op jit(solution)/shard_map/jit(_where)/select_n | solution.py:18
  27.5 0.0 copy-start
  27.5 0.0 all-reduce.6.cloned.1.call-update
  27.6 0.7 copy-done
  28.3 53.1 %all-gather = bf16[16,4,4096]{2,1,0:T(4,128)(2,1)S(1)} all-gather(bf16[1,4,4096]{2,1,0:T(4,128)(2,1)S(1)} %copy-done), channel_id=2, replica_groups=mesh['replica'=2,'shard'=16] {'shard'}, dimensions={0}, use_global_device_ids=true | all-gather | bytes 557056 | tf_op jit(solution)/shard_map/all_gather | solution.py:58
  81.4 0.1 squeeze_reshape.3
  81.5 0.0 copy-start.1
  81.6 0.0 all-reduce.4.cloned.1.call-done
  81.6 32.0 %multiply_subtract_fusion = (f32[960,4096]{1,0:T(8,128)}, f32[960,4096]{1,0:T(8,128)}) fusion(f32[960,4096]{1,0:T(8,128)} %param.10, f32[960,4096]{1,0:T(8,128)} %all-reduce.4.cloned.1.call-done, f32[960,4096]{1,0:T(8,128)} %param.11), kind=kLoop, calls=%fused_computation.11 | loop fusion | flops 23592960 | bytes 78643200 | tf_op jit(solution)/shard_map/sub | solution.py:47
  113.6 25.9 %all-reduce.6.cloned.1.call-done = (bf16[1,960,4096]{2,1,0:T(8,128)(2,1)}, bf16[1,960,4096]{2,1,0:T(8,128)(2,1)}) async-done(((bf16[1,960,4096]{2,1,0:T(8,128)(2,1)}, bf16[1,960,4096]{2,1,0:T(8,128)(2,1)}), (bf16[1,960,4096]{2,1,0:T(8,128)(2,1)}, bf16[1,960,4096]{2,1,0:T(8,128)(2,1)})) %all-reduce.6.cloned.1.call-update) | async-done | bytes 15728656 | tf_op jit(solution)/shard_map/psum | solution.py:19
  139.5 0.0 copy-done.1
  139.5 35.2 %fusion.6 = f32[1,960,4096]{2,1,0:T(8,128)} fusion(f32[960,4096]{1,0:T(8,128)} %get-tuple-element.5, bf16[1,960,4096]{2,1,0:T(8,128)(2,1)} %get-tuple-element.3, bf16[1,960,4096]{2,1,0:T(8,128)(2,1)} %param.13, bf16[1,960,4096]{2,1,0:T(8,128)(2,1)} %get-tuple-element.4, bf16[1,960,4096]{2,1,0:T(8,128)(2,1)} %param.12, pred[]{:T(512)S(6)} %eq.7, ...), kind=kOutput, calls=%fused_computation.8 | convolution fusion | flops 1082019840 | bytes 63561728 | tf_op jit(solution)/shard_map/dot_general | solution.py:66
Async XLA Ops:
  7.2 74.4 %all-reduce.4.cloned.1.call-start = ((), (), s32[]{:S(2)}) async-start(), calls=%async_computation | async-start | bytes 31457280 | tf_op jit(solution)/shard_map/psum | solution.py:44
  21.1 118.4 %all-reduce.6.cloned.1.call-start = ((), (), s32[]{:S(2)}) async-start(), calls=%async_computation.1 | async-start | bytes 31457280 | tf_op jit(solution)/shard_map/psum | solution.py:19
  27.5 0.8 copy-start
  81.5 57.9 %copy-start.1 = (bf16[1,960,64]{1,2,0:T(8,128)(2,1)S(1)}, bf16[1,960,64]{1,2,0:T(8,128)(2,1)}, u32[]{:S(2)}) copy-start(bf16[1,960,64]{1,2,0:T(8,128)(2,1)} %param.15) | copy-start | bytes 368644
Sparse Core Ops, SparseCore 0:
  21.2 58.5 all-reduce.3
  82.4 57.0 all-reduce.5
